TPU v7x, 32 devices: a whole 2x2x4 slice. The times are simulated.
32 devices in a mesh: groups: 1, rows: 16 (over z, y, core), heads: 2 (over x).
Axes of the slice: x: 2, y: 2, z: 4, core: 2. Of those that a mesh axis runs over, the one named last changes fastest.
Arguments:
- queries: bfloat16 [2048, 8192], P(('groups', 'rows'), 'heads'), may hold values from -40 to 40
- passages: bfloat16 [768, 1024], P(('groups', 'rows')), may hold values from -6 to 6
- enc_gain: bfloat16 [1024], replicated, may hold values from 0.099609375 to 1.8984375
- key_weight: bfloat16 [1024, 8192], P(None, 'heads'), may hold values from -0.1875 to 0.1875
- value_weight: bfloat16 [1024, 8192], P(None, 'heads'), may hold values from -0.1875 to 0.1875
- out_weight: bfloat16 [8192, 1024], P('heads'), may hold values from -0.125 to 0.125
- passage_length: int32 [3], P('groups'), may hold values from 64 to 256, as said below
Outputs:
- cross_out: bfloat16 [2048, 1024], P(('groups', 'rows'))
Inputs may be any that keep to these rules, and one draw needn't show every extreme that they name: `passage_length`: every passage has at least a quarter of its padded tokens; some passage is full and some has exactly 64 tokens.
All inputs are finite; a program needn't handle non-finite values.
Results may differ from a plain program's by a relative error of at most 0.012.
The roundings to bfloat16 on the way count: a program that leaves them out, or rounds other values in their place, can miss the bound.
Values may be sent and summed in bfloat16 or wider, within the bound.
A program may use at most 128 MiB of HBM per device.

v0:
```python
import functools

import jax
import jax.numpy as jnp
from jax import lax
from jax.experimental import pallas as pl
from jax.experimental.pallas import tpu as pltpu
from jax.sharding import PartitionSpec as P

DK = 128
PASS_LEN = 256
SHORT_LEN = PASS_LEN // 4
LOWEST = -1e30
MESH = pl.DeviceIdType.MESH
LOADS = 4
GROUP = 2 * DK
OUT_CHUNK = 512


def flip(index, bits):
    bit = 1
    while bit <= bits:
        if bits & bit:
            index = index + bit - 2 * bit * ((index // bit) % 2)
        bit *= 2
    return index


def kernel(
    n_rows,
    n_heads,
    length_ref,
    queries_ref,
    passages_ref,
    gain_ref,
    key_ref,
    value_ref,
    outw_ref,
    out_ref,
    rows_all,
    norm_all,
    normed,
    query_buf,
    key_w,
    value_w,
    out_w,
    keys,
    values,
    attended,
    core_send,
    core_recv,
    own_part,
    x_parts,
    local_sem,
    load_sem,
    z_send_sem,
    y_send_sem,
    x_send_sem,
    core_send_sem,
    main_recv,
    rest_recv,
    query_sem,
    out_core_sem,
    out_x_sem,
):
    block, width = passages_ref.shape
    dec, inner = queries_ref.shape
    half = inner // 2
    n_pass = length_ref.shape[0]
    n_z = n_rows // 4
    wide = width * 4 // 8
    narrow = width - wide

    me = lax.axis_index("rows")
    x = lax.axis_index("heads")
    core = me % 2
    y = (me // 2) % 2
    z = me // 4

    def row_of(z_, y_, c_):
        return (z_ * 2 + y_) * 2 + c_

    def at_row(r):
        return {"rows": r}

    partner = at_row(flip(me, 1))
    across_y = at_row(flip(me, 2))
    side = x % 2
    x_peers = [{"heads": flip(x, d)} for d in range(1, n_heads)]
    across_x = x_peers[0]

    def rows_at(r):
        return pl.ds(pl.multiple_of(r * block, 16), block)

    main_cols = pl.ds(pl.multiple_of(side * narrow, 128), wide)
    rest_cols = pl.ds(pl.multiple_of((1 - side) * wide, 128), narrow)
    give_cols = pl.ds(pl.multiple_of(side * wide, 128), narrow)

    own_rows = pltpu.make_async_copy(passages_ref, rows_all.at[rows_at(me)], local_sem.at[0])
    own_rows.start()
    mine = pl.ds(pl.multiple_of(core * half, 128), half)
    theirs = pl.ds(pl.multiple_of((1 - core) * half, 128), half)
    my_t = pl.ds(pl.multiple_of(core * dec, 128), dec)
    own_queries = pltpu.make_async_copy(
        queries_ref.at[:, mine], query_buf.at[my_t], local_sem.at[1]
    )
    own_queries.start()
    loads = []
    share = half // LOADS
    for part in range(LOADS):
        here = pl.ds(part * share, share)
        there = pl.ds(pl.multiple_of(core * half + part * share, 128), share)
        loads.append(
            (
                pltpu.make_async_copy(
                    key_ref.at[:, there], key_w.at[:, here], load_sem.at[0, part]
                ),
                pltpu.make_async_copy(
                    value_ref.at[:, there], value_w.at[:, here], load_sem.at[1, part]
                ),
                pltpu.make_async_copy(outw_ref.at[there], out_w.at[here], load_sem.at[2, part]),
            )
        )

    barrier = pltpu.get_barrier_semaphore()
    z_peers = [row_of(flip(z, d), y, core) for d in range(1, n_z)]
    peers = [at_row(r) for r in z_peers] + [across_y, partner] + x_peers
    for peer in peers:
        pl.semaphore_signal(barrier, inc=1, device_id=peer, device_id_type=MESH)
    pl.semaphore_wait(barrier, len(peers))

    sent = []

    def send(src, dst, send_sem, recv_sem, to):
        copy = pltpu.make_async_remote_copy(
            src_ref=src, dst_ref=dst, send_sem=send_sem, recv_sem=recv_sem,
            device_id=to, device_id_type=MESH,
        )
        copy.start()
        sent.append(copy)

    def send_block(r, cols, send_sem, recv_sem, to):
        view = rows_all.at[rows_at(r), cols]
        send(view, view, send_sem, recv_sem.at[r], to)

    def await_block(r, cols, recv_sem):
        view = rows_all.at[rows_at(r), cols]
        pltpu.make_async_copy(view, view, recv_sem.at[r]).wait()

    def send_own(cols, send_sem, recv_sem, to):
        send(
            passages_ref.at[:, cols], rows_all.at[rows_at(me), cols], send_sem, recv_sem.at[me], to
        )

    for d in range(1, n_z):
        send_own(main_cols, z_send_sem.at[d - 1], main_recv, at_row(z_peers[d - 1]))
    send_own(main_cols, y_send_sem.at[0], main_recv, across_y)
    send_own(main_cols, core_send_sem.at[0, 0], main_recv, partner)
    send_own(rest_cols, core_send_sem.at[1, 0], rest_recv, partner)
    send(
        queries_ref.at[:, theirs], query_buf.at[my_t], query_sem.at[0], query_sem.at[1], partner
    )
    for triple in loads:
        triple[0].start()
        triple[1].start()
    for triple in loads:
        triple[2].start()

    others = []
    from_y = row_of(z, 1 - y, core)
    order = [("y", from_y, 0)]
    for d in range(1, n_z):
        order.append(("z", z_peers[d - 1], d))
        if d > 1:
            order.append(("y", row_of(flip(z, d - 1), 1 - y, core), d - 1))
    order.append(("y", row_of(flip(z, n_z - 1), 1 - y, core), n_z - 1))
    for number, (kind, r, d) in enumerate(order):
        await_block(r, main_cols, main_recv)
        if kind == "z":
            send_block(r, main_cols, y_send_sem.at[d], main_recv, across_y)
        send_block(r, give_cols, x_send_sem.at[number], rest_recv, across_x)
        send_block(r, main_cols, core_send_sem.at[0, number + 1], main_recv, partner)
        others.append(r)
    gain = gain_ref[...].astype(jnp.float32).reshape(1, width)

    def normalize(r):
        wide_rows = rows_all[rows_at(r), :].astype(jnp.float32)
        mean_square = jnp.mean(wide_rows * wide_rows, axis=-1, keepdims=True)
        norm_all[rows_at(r), :] = (
            wide_rows * lax.rsqrt(mean_square + 1e-06) * gain
        ).astype(jnp.bfloat16)

    def normalize_partner(r):
        await_block(flip(r, 1), main_cols, main_recv)
        await_block(flip(r, 1), rest_cols, rest_recv)
        normalize(flip(r, 1))

    own_rows.wait()
    normalize(me)
    normalize_partner(me)
    for number, r in enumerate(others):
        await_block(r, rest_cols, rest_recv)
        send_block(r, rest_cols, core_send_sem.at[1, number + 1], rest_recv, partner)
        normalize(r)
        if number:
            normalize_partner(others[number - 1])
    normalize_partner(others[-1])

    lengths = [length_ref[p] for p in range(n_pass)]
    is_short = []
    open_still = jnp.int32(1)
    for p in range(n_pass):
        hit = open_still * (lengths[p] == SHORT_LEN).astype(jnp.int32)
        is_short.append(hit)
        open_still = open_still - hit
    passed = []
    seen = jnp.int32(0)
    for p in range(n_pass):
        seen = seen + is_short[p]
        passed.append(seen)
    sizes = [PASS_LEN] * (n_pass - 1) + [SHORT_LEN]
    number = sum(sizes)
    offsets = lax.broadcasted_iota(jnp.int32, (1, number), 1)
    bias = jnp.zeros((1, number), jnp.float32)

    def lanes(flag, shape):
        return jnp.full(shape, flag, jnp.int32) == 1

    step = SHORT_LEN
    for p in range(n_pass - 1):
        length = lengths[p] + passed[p] * (lengths[p + 1] - lengths[p])
        bad = (offsets >= p * PASS_LEN + length) & (offsets < (p + 1) * PASS_LEN)
        bias = jnp.where(bad, LOWEST, bias)
        moved = lanes(passed[p], (step, width))
        for row in range(p * PASS_LEN, (p + 1) * PASS_LEN, step):
            here = norm_all[row : row + step, :].astype(jnp.float32)
            after = norm_all[row + PASS_LEN : row + PASS_LEN + step, :].astype(jnp.float32)
            normed[row : row + step, :] = jnp.where(moved, after, here).astype(jnp.bfloat16)
    last = norm_all[0:step, :].astype(jnp.float32)
    for p in range(1, n_pass):
        place = p * PASS_LEN
        here = norm_all[place : place + step, :].astype(jnp.float32)
        last = jnp.where(lanes(is_short[p], (step, width)), here, last)
    normed[number - step : number, :] = last.astype(jnp.bfloat16)

    for triple in loads:
        triple[0].wait()
        triple[1].wait()
    own_queries.wait()
    other_t = pl.ds(pl.multiple_of((1 - core) * dec, 128), dec)
    pltpu.make_async_copy(query_buf.at[other_t], query_buf.at[other_t], query_sem.at[1]).wait()

    groups = half // GROUP

    def project(g):
        cols = slice(g * GROUP, (g + 1) * GROUP)
        keys[:, cols] = jnp.dot(
            normed[...], key_w[:, cols], preferred_element_type=jnp.float32
        ).astype(jnp.bfloat16)
        values[:, cols] = jnp.dot(
            normed[...], value_w[:, cols], preferred_element_type=jnp.float32
        ).astype(jnp.bfloat16)

    def attend(g, low, high):
        size = high - low
        for h in range(GROUP // DK):
            cols = slice(g * GROUP + h * DK, g * GROUP + (h + 1) * DK)
            asked = jnp.concatenate(
                [query_buf[low:high, cols], query_buf[dec + low : dec + high, cols]], axis=0
            )
            scores = lax.dot_general(
                asked,
                keys[:, cols],
                (((1,), (1,)), ((), ())),
                preferred_element_type=jnp.float32,
            )
            scores = scores + bias
            top = jnp.max(scores, axis=-1, keepdims=True)
            expo = jnp.exp(scores - top)
            denom = jnp.sum(expo, axis=-1, keepdims=True)
            mixed = jnp.dot(
                expo.astype(jnp.bfloat16),
                values[:, cols],
                preferred_element_type=jnp.float32,
            )
            mixed = (mixed / denom).astype(jnp.bfloat16)
            attended[low:high, cols] = mixed[:size]
            attended[dec + low : dec + high, cols] = mixed[size:]

    chunks = width // OUT_CHUNK

    def chunk_of(j):
        return slice(j * OUT_CHUNK, (j + 1) * OUT_CHUNK)

    def core_rows(c, low, high):
        return pl.ds(pl.multiple_of(c * dec + low, 16), high - low)

    def to_core(n, low, high):
        rows = slice(low, high)
        for j in range(chunks):
            cols = chunk_of(j)
            core_send[rows, cols] = jnp.dot(
                attended[core_rows(1 - core, low, high), :],
                out_w[:, cols],
                preferred_element_type=jnp.float32,
            ).astype(jnp.bfloat16)
            send(
                core_send.at[rows, cols], core_recv.at[rows, cols], out_core_sem.at[0, n, j],
                out_core_sem.at[1, n, j], partner,
            )
        for j in range(chunks):
            cols = chunk_of(j)
            own_part[rows, cols] = jnp.dot(
                attended[core_rows(core, low, high), :],
                out_w[:, cols],
                preferred_element_type=jnp.float32,
            )

    def to_x(n, low, high):
        rows = slice(low, high)
        for j in range(chunks):
            cols = chunk_of(j)
            view = core_recv.at[rows, cols]
            pltpu.make_async_copy(view, view, out_core_sem.at[1, n, j]).wait()
            x_parts[x, rows, cols] = (
                own_part[rows, cols] + core_recv[rows, cols].astype(jnp.float32)
            ).astype(jnp.bfloat16)
            view = x_parts.at[x, rows, cols]
            for d, peer in enumerate(x_peers):
                send(view, view, out_x_sem.at[0, n, d, j], out_x_sem.at[1, n, d, j], peer)

    def finish(n, low, high):
        rows = slice(low, high)
        for j in range(chunks):
            cols = chunk_of(j)
            for d in range(1, n_heads):
                view = x_parts.at[flip(x, d), rows, cols]
                pltpu.make_async_copy(view, view, out_x_sem.at[1, n, d - 1, j]).wait()
            total = x_parts[0, rows, cols].astype(jnp.float32)
            for term in range(1, n_heads):
                total += x_parts[term, rows, cols].astype(jnp.float32)
            out_ref[rows, cols] = total.astype(jnp.bfloat16)

    project(0)
    for g in range(groups):
        if g + 1 < groups:
            project(g + 1)
        attend(g, 0, dec)
    for triple in loads:
        triple[2].wait()
    to_core(0, 0, dec)
    to_x(0, 0, dec)
    finish(0, 0, dec)
    for copy in sent:
        copy.wait_send()


def on_device(
    n_rows, n_heads, queries, passages, enc_gain, key_weight, value_weight, out_weight, passage_length
):
    dec, inner = queries.shape
    block, width = passages.shape
    half = inner // 2
    n_pass = passage_length.shape[0]
    number = (n_pass - 1) * PASS_LEN + SHORT_LEN
    n_z = n_rows // 4
    same = n_rows // 2
    chunks = width // OUT_CHUNK
    bf16 = jnp.bfloat16
    dma = pltpu.SemaphoreType.DMA
    vmem = pl.BlockSpec(memory_space=pltpu.VMEM)
    anywhere = pl.BlockSpec(memory_space=pl.ANY)
    return pl.pallas_call(
        functools.partial(kernel, n_rows, n_heads),
        out_shape=jax.ShapeDtypeStruct((dec, width), bf16),
        in_specs=[
            pl.BlockSpec(memory_space=pltpu.SMEM),
            anywhere,
            anywhere,
            vmem,
            anywhere,
            anywhere,
            anywhere,
        ],
        out_specs=vmem,
        scratch_shapes=[
            pltpu.VMEM((n_rows * block, width), bf16),
            pltpu.VMEM((n_rows * block, width), bf16),
            pltpu.VMEM((number, width), bf16),
            pltpu.VMEM((2 * dec, half), bf16),
            pltpu.VMEM((width, half), bf16),
            pltpu.VMEM((width, half), bf16),
            pltpu.VMEM((half, width), bf16),
            pltpu.VMEM((number, half), bf16),
            pltpu.VMEM((number, half), bf16),
            pltpu.VMEM((2 * dec, half), bf16),
            pltpu.VMEM((dec, width), bf16),
            pltpu.VMEM((dec, width), bf16),
            pltpu.VMEM((dec, width), jnp.float32),
            pltpu.VMEM((n_heads, dec, width), bf16),
            dma((2,)),
            dma((3, LOADS)),
            dma((n_z - 1,)),
            dma((n_z,)),
            dma((same,)),
            dma((2, same)),
            dma((n_rows,)),
            dma((n_rows,)),
            dma((2,)),
            dma((2, 1, chunks)),
            dma((2, 1, n_heads - 1, chunks)),
        ],
        compiler_params=pltpu.CompilerParams(
            collective_id=0, has_side_effects=True, vmem_limit_bytes=60 * 1024 * 1024
        ),
    )(
        passage_length,
        queries,
        passages,
        enc_gain,
        key_weight,
        value_weight,
        out_weight,
    )


def solution(mesh):
    return jax.shard_map(
        functools.partial(on_device, mesh.shape["rows"], mesh.shape["heads"]),
        mesh=mesh,
        in_specs=(
            P(("groups", "rows"), "heads"),
            P(("groups", "rows"), None),
            P(),
            P(None, "heads"),
            P(None, "heads"),
            P("heads", None),
            P("groups"),
        ),
        out_specs=P(("groups", "rows"), None),
        check_vma=False,
    )
```

profile of v0, /device:TPU:0, one launch (start us, length us, event | category | flops | bytes accessed | tf_op | source)
XLA Modules:
  0.0 45.4 jit_solution(17072077748049386612)
XLA Ops:
  0.0 43.7 %shard_map.73 = bf16[128,1024]{1,0:T(8,128)(2,1)} custom-call(s32[3]{0:T(128)} %length_ref.1, bf16[128,4096]{1,0:T(8,128)(2,1)} %queries_ref.1, bf16[48,1024]{1,0:T(8,128)(2,1)} %passages_ref.1, bf16[1024]{0:T(1024)(128)(2,1)} %gain_ref.1, bf16[1024,4096]{1,0:T(8,128)(2,1)} %key_ref.1, bf16[1024,4096]{1,0:T(8,128)(2,1)} %value_ref.1, bf16[4096,1024]{1,0:T(8,128)(2,1)} %outw_ref.1), custom_call_target="tpu_custom_call" | custom-call | tf_op jit(solution)/shard_map/pallas_call | solution.py:373
  43.7 1.7 %copy.9 = bf16[128,1024]{1,0:T(8,128)(2,1)} copy(bf16[128,1024]{1,0:T(8,128)(2,1)} %shard_map.73) | data formatting | bytes 524288
where the time goes:
time: 45.6 us; the launch traced here: 45.4 us
  Pallas kernels  43.7 us (96%)
  local copies, waits for them, and re-layouts  1.67 us (4%)
    pallas_call x1, Pallas kernels, on_device(): pl.pallas_call(functools.partial(kernel, n_rows, n_heads), out_shape=jax....  43.7 us
    unnamed x1, local copies, waits for them, and re-layouts  1.67 us

commit v1 on v0

v1 whole, which is shorter than its diff:
```python
import functools

import jax
import jax.numpy as jnp
from jax import lax
from jax.experimental import pallas as pl
from jax.experimental.pallas import tpu as pltpu
from jax.sharding import PartitionSpec as P

DK = 128
PASS_LEN = 256
SHORT_LEN = PASS_LEN // 4
LOWEST = -1e30
MESH = pl.DeviceIdType.MESH
LOADS = 4
GROUP = 256
OUT_CHUNK = 512
ROW_BLOCK = 16
GIVE, SHARED, REST = 0, 1, 2
SPLITS = 2


def flip(index, bits):
    bit = 1
    while bit <= bits:
        if bits & bit:
            index = index + bit - 2 * bit * ((index // bit) % 2)
        bit *= 2
    return index


def kernel(
    n_rows,
    n_heads,
    length_ref,
    queries_ref,
    passages_ref,
    gain_ref,
    key_ref,
    value_ref,
    outw_ref,
    out_ref,
    own_raw,
    rows,
    query_buf,
    key_w,
    value_w,
    out_w,
    keys,
    values,
    key_sum,
    value_sum,
    score_buf,
    weight_buf,
    attended,
    core_send,
    core_recv,
    own_part,
    x_parts,
    local_sem,
    load_sem,
    send_sem,
    recv_sem,
    query_sem,
    out_core_sem,
    out_x_sem,
):
    block, width = passages_ref.shape
    dec, inner = queries_ref.shape
    half = inner // 2
    n_pass = length_ref.shape[0]
    n_z = n_rows // 4
    quarter = width // 4
    middle = width - 2 * quarter
    bf16 = jnp.bfloat16
    f32 = jnp.float32

    me = lax.axis_index("rows")
    x = lax.axis_index("heads")
    core = me % 2
    y = (me // 2) % 2
    z = me // 4
    side = x % 2

    def at_row(r):
        return {"rows": r}

    partner = at_row(flip(me, 1))
    across_y = at_row(flip(me, 2))
    z_peers = [at_row(flip(me, 4 * d)) for d in range(1, n_z)]
    x_peers = [{"heads": flip(x, d)} for d in range(1, n_heads)]
    across_x = x_peers[0]

    own_rows = pltpu.make_async_copy(passages_ref, own_raw, local_sem.at[0])
    own_rows.start()
    barrier = pltpu.get_barrier_semaphore()
    peers = z_peers + [across_y, partner] + x_peers
    for peer in peers:
        pl.semaphore_signal(barrier, inc=1, device_id=peer, device_id_type=MESH)

    mine = pl.ds(pl.multiple_of(core * half, 128), half)
    theirs = pl.ds(pl.multiple_of((1 - core) * half, 128), half)
    share = half // LOADS
    loads = []
    for part in range(LOADS):
        here = pl.ds(part * share, share)
        there = pl.ds(pl.multiple_of(core * half + part * share, 128), share)
        loads.append(
            (
                pltpu.make_async_copy(
                    key_ref.at[:, there], key_w.at[:, here], load_sem.at[0, part]
                ),
                pltpu.make_async_copy(
                    value_ref.at[:, there], value_w.at[:, here], load_sem.at[1, part]
                ),
                pltpu.make_async_copy(outw_ref.at[there], out_w.at[here], load_sem.at[2, part]),
            )
        )
    own_queries = pltpu.make_async_copy(
        queries_ref.at[:, mine], query_buf.at[0:dec], local_sem.at[1]
    )

    def slot_of(dy, dz):
        return dy * n_z + dz

    def place(slot, c):
        return pl.ds(pl.multiple_of(slot * 2 * block + c * block, 16), block)

    give_at = pl.multiple_of(side * (width - quarter), 128)
    rest_at = pl.multiple_of((1 - side) * (width - quarter), 128)
    main_at = pl.multiple_of(side * quarter, 128)
    main_cols = pl.ds(main_at, width - quarter)
    rest_cols = pl.ds(rest_at, quarter)
    cols_of = {GIVE: pl.ds(give_at, quarter), SHARED: pl.ds(quarter, middle), REST: rest_cols}

    def unit_of(slot, c, kind):
        return rows.at[place(slot, c), cols_of[kind]]

    def whole_of(slot, c):
        return rows.at[place(slot, c)]

    own_rows.wait()
    for triple in loads:
        triple[0].start()
        triple[1].start()
    own_queries.start()
    for triple in loads:
        triple[2].start()
    wide_rows = own_raw[...].astype(f32)
    mean_square = jnp.mean(wide_rows * wide_rows, axis=-1, keepdims=True)
    gain = gain_ref[...].astype(f32).reshape(1, width)
    rows[place(0, core), :] = (wide_rows * lax.rsqrt(mean_square + 1e-06) * gain).astype(bf16)

    pl.semaphore_wait(barrier, len(peers))

    sent = []

    def send(src, dst, send_at, recv_at, to):
        copy = pltpu.make_async_remote_copy(
            src_ref=src, dst_ref=dst, send_sem=send_at, recv_sem=recv_at,
            device_id=to, device_id_type=MESH,
        )
        copy.start()
        sent.append(copy)

    count = [0]

    def next_sem():
        count[0] += 1
        return send_sem.at[count[0] - 1]

    def send_unit(slot, kind, to, there_slot, there_kind):
        send(
            unit_of(slot, core, kind),
            unit_of(there_slot, core, kind),
            next_sem(),
            recv_sem.at[there_slot, core, there_kind],
            to,
        )

    def await_unit(slot, c, kind):
        view = unit_of(slot, c, kind)
        pltpu.make_async_copy(view, view, recv_sem.at[slot, c, kind]).wait()

    for kind in (GIVE, SHARED):
        for d in range(n_z - 1, 0, -1):
            send_unit(0, kind, z_peers[d - 1], slot_of(0, d), kind)
        send_unit(0, kind, across_y, slot_of(1, 0), kind)
    send(whole_of(0, core), whole_of(0, core), next_sem(), recv_sem.at[0, core, 0], partner)
    send(
        queries_ref.at[:, theirs], query_buf.at[dec : 2 * dec], query_sem.at[0], query_sem.at[1], partner
    )

    def relay(slot, kind, over_y):
        await_unit(slot, core, kind)
        if over_y:
            send_unit(slot, kind, across_y, slot + n_z, kind)
        if kind == GIVE:
            send_unit(slot, kind, across_x, slot, REST)
        send_unit(slot, kind, partner, slot, kind)

    groups = half // GROUP
    waited = set()

    def weights_for(g):
        part = g * GROUP // share
        if part not in waited:
            waited.add(part)
            loads[part][0].wait()
            loads[part][1].wait()

    def keep(slots, cols, made_keys, made_values):
        made_keys = made_keys.astype(bf16)
        made_values = made_values.astype(bf16)
        for number, slot in enumerate(slots):
            dy, dz = slot // n_z, slot % n_z
            chip = flip(z, dz) * 2 + flip(y, dy)
            to = pl.ds(pl.multiple_of(chip * 2 * block, 16), 2 * block)
            part = slice(number * 2 * block, (number + 1) * 2 * block)
            keys[to, cols] = made_keys[part]
            values[to, cols] = made_values[part]

    def rows_in(slots):
        return slice(slots[0] * 2 * block, (slots[-1] + 1) * 2 * block)

    def project(slots, g):
        weights_for(g)
        cols = slice(g * GROUP, (g + 1) * GROUP)
        chunk = rows[rows_in(slots), :]
        keep(
            slots,
            cols,
            jnp.dot(chunk, key_w[:, cols], preferred_element_type=f32),
            jnp.dot(chunk, value_w[:, cols], preferred_element_type=f32),
        )

    def project_main(slots, g):
        cols = slice(g * GROUP, (g + 1) * GROUP)
        chunk = rows[rows_in(slots), main_cols]
        here = slice(0, len(slots) * 2 * block)
        key_sum[here, cols] = jnp.dot(chunk, key_w[main_cols, cols], preferred_element_type=f32)
        value_sum[here, cols] = jnp.dot(chunk, value_w[main_cols, cols], preferred_element_type=f32)

    def project_rest(slots, g):
        cols = slice(g * GROUP, (g + 1) * GROUP)
        chunk = rows[rows_in(slots), rest_cols]
        here = slice(0, len(slots) * 2 * block)
        keep(
            slots,
            cols,
            key_sum[here, cols]
            + jnp.dot(chunk, key_w[rest_cols, cols], preferred_element_type=f32),
            value_sum[here, cols]
            + jnp.dot(chunk, value_w[rest_cols, cols], preferred_element_type=f32),
        )

    def interleave(pieces, events, each):
        events = list(events)
        for piece in pieces:
            piece()
            for event in events[:each]:
                event()
            events = events[each:]
        for event in events:
            event()

    def pieces_of(work, slots):
        return [functools.partial(work, slots, g) for g in range(groups)]

    near = list(range(n_z - 1, 0, -1))
    line = [slot_of(0, d) for d in near]
    other = [slot_of(1, d) for d in near]
    beside = slot_of(1, 0)

    def from_partner(slots, kinds):
        for slot in slots:
            for kind in kinds:
                await_unit(slot, 1 - core, kind)

    R = functools.partial
    relay(beside, GIVE, False)
    view = whole_of(0, 1 - core)
    pltpu.make_async_copy(view, view, recv_sem.at[0, 1 - core, 0]).wait()
    events = [R(relay, beside, SHARED, False)]
    events += [R(relay, s, GIVE, True) for s in line]
    events += [R(relay, beside, REST, False)]
    events += [R(relay, s, SHARED, True) for s in line]
    interleave(pieces_of(project, [0]), events, 1)
    from_partner([beside], (GIVE, SHARED, REST))
    events = []
    for s, o in zip(line, other):
        events += [R(relay, o, GIVE, False), R(relay, s, REST, False)]
    interleave(pieces_of(project, [beside]), events, 2)
    from_partner(line, (GIVE, SHARED, REST))
    events = [R(relay, o, SHARED, False) for o in other]
    events += [R(relay, o, REST, False) for o in other]
    interleave(pieces_of(project, line[::-1]), events, 1)
    from_partner(other, (GIVE, SHARED))
    interleave(pieces_of(project_main, other[::-1]), [], 1)
    from_partner(other, (REST,))
    for piece in pieces_of(project_rest, other[::-1]):
        piece()

    lengths = [length_ref[p] for p in range(n_pass)]
    short_at = jnp.int32(0)
    full_at = jnp.int32(0)
    short_open = jnp.int32(1)
    full_open = jnp.int32(1)
    for p in range(n_pass):
        hit = short_open * (lengths[p] == SHORT_LEN).astype(jnp.int32)
        short_at = short_at + hit * p
        short_open = short_open - hit
        hit = full_open * (lengths[p] == PASS_LEN).astype(jnp.int32)
        full_at = full_at + hit * p
        full_open = full_open - hit
    starts = [full_at]
    tails = []
    for j in range(n_pass - 2):
        low = short_at + (full_at < short_at).astype(jnp.int32) * (full_at - short_at)
        high = short_at + full_at - low
        at = j + (j >= low).astype(jnp.int32)
        at = at + (at >= high).astype(jnp.int32)
        starts.append(at)
        length = jnp.int32(0)
        for p in range(n_pass):
            length = length + (at == p).astype(jnp.int32) * lengths[p]
        offsets = lax.broadcasted_iota(jnp.int32, (1, PASS_LEN), 1)
        tails.append(jnp.where(offsets < length, 0.0, LOWEST).astype(f32))
    starts = [at * PASS_LEN for at in starts]
    short_start = short_at * PASS_LEN
    kept = (n_pass - 1) * PASS_LEN + SHORT_LEN
    number = kept + SHORT_LEN

    own_queries.wait()
    view = query_buf.at[dec : 2 * dec]
    pltpu.make_async_copy(view, view, query_sem.at[1]).wait()

    heads = half // DK
    counted = jnp.concatenate(
        [jnp.ones((kept, DK), bf16), jnp.zeros((SHORT_LEN, DK), bf16)], axis=0
    )

    def head_cols(h):
        return slice(h * DK, (h + 1) * DK)

    def score(h, low, high):
        cols = head_cols(h)
        asked = jnp.concatenate([query_buf[low:high, cols], query_buf[dec + low : dec + high, cols]], axis=0)
        last = keys[pl.ds(short_start, SHORT_LEN), cols]
        against = jnp.concatenate(
            [keys[pl.ds(at, PASS_LEN), cols] for at in starts] + [last, last], axis=0
        )
        score_buf[h % 2] = lax.dot_general(
            asked, against, (((1,), (1,)), ((), ())), preferred_element_type=f32
        )

    def weigh(h, low, high):
        for row in range(0, 2 * (high - low), ROW_BLOCK):
            here = slice(row, row + ROW_BLOCK)
            scores = score_buf[h % 2, here, :]
            scores = jnp.concatenate(
                [scores[:, :PASS_LEN]]
                + [
                    scores[:, (j + 1) * PASS_LEN : (j + 2) * PASS_LEN] + tails[j]
                    for j in range(n_pass - 2)
                ]
                + [scores[:, (n_pass - 1) * PASS_LEN :]],
                axis=1,
            )
            top = jnp.max(scores, axis=-1, keepdims=True)
            weight_buf[h % 2, here, :] = jnp.exp(scores - top).astype(bf16)

    def mix(h, low, high):
        cols = head_cols(h)
        size = high - low
        taken = jnp.concatenate(
            [values[pl.ds(at, PASS_LEN), cols] for at in starts]
            + [values[pl.ds(short_start, SHORT_LEN), cols], jnp.zeros((SHORT_LEN, DK), bf16)],
            axis=0,
        )
        taken = jnp.concatenate([taken, counted], axis=1)
        mixed = jnp.dot(weight_buf[h % 2], taken, preferred_element_type=f32)
        mixed = (mixed[:, :DK] / mixed[:, DK:]).astype(bf16)
        attended[low:high, cols] = mixed[:size]
        attended[dec + low : dec + high, cols] = mixed[size:]

    def attend(low, high, hooks):
        for step in range(heads + 2):
            if step < heads:
                score(step, low, high)
            if 0 < step < heads + 1:
                weigh(step - 1, low, high)
            if 1 < step:
                mix(step - 2, low, high)
            if step in hooks:
                hooks[step]()

    chunks = width // OUT_CHUNK

    def chunk_of(j):
        return slice(j * OUT_CHUNK, (j + 1) * OUT_CHUNK)

    def to_core(n, low, high):
        here = slice(low, high)
        size = high - low
        mixed = jnp.concatenate([attended[low:high, :], attended[dec + low : dec + high, :]], axis=0)
        for j in range(chunks):
            cols = chunk_of(j)
            made = jnp.dot(mixed, out_w[:, cols], preferred_element_type=f32)
            core_send[here, cols] = made[size:].astype(bf16)
            send(
                core_send.at[here, cols], core_recv.at[here, cols], out_core_sem.at[0, n, j],
                out_core_sem.at[1, n, j], partner,
            )
            own_part[here, cols] = made[:size]

    def to_x(n, low, high):
        here = slice(low, high)
        for j in range(chunks):
            cols = chunk_of(j)
            view = core_recv.at[here, cols]
            pltpu.make_async_copy(view, view, out_core_sem.at[1, n, j]).wait()
            x_parts[x, here, cols] = (
                own_part[here, cols] + core_recv[here, cols].astype(f32)
            ).astype(bf16)
            view = x_parts.at[x, here, cols]
            for d, peer in enumerate(x_peers):
                send(view, view, out_x_sem.at[0, n, d, j], out_x_sem.at[1, n, d, j], peer)

    def finish(n, low, high):
        here = slice(low, high)
        for j in range(chunks):
            cols = chunk_of(j)
            for d in range(1, n_heads):
                view = x_parts.at[flip(x, d), here, cols]
                pltpu.make_async_copy(view, view, out_x_sem.at[1, n, d - 1, j]).wait()
            total = x_parts[0, here, cols].astype(f32)
            for term in range(1, n_heads):
                total += x_parts[term, here, cols].astype(f32)
            out_ref[here, cols] = total.astype(bf16)

    size = dec // SPLITS
    bounds = [(n * size, (n + 1) * size) for n in range(SPLITS)]
    for n, (low, high) in enumerate(bounds):
        hooks = {}
        if n:
            hooks[5] = functools.partial(to_x, n - 1, *bounds[n - 1])
        attend(low, high, hooks)
        if not n:
            for triple in loads:
                triple[2].wait()
        to_core(n, low, high)
    to_x(SPLITS - 1, *bounds[-1])
    for n, (low, high) in enumerate(bounds):
        finish(n, low, high)
    for copy in sent:
        copy.wait_send()


def on_device(
    n_rows, n_heads, queries, passages, enc_gain, key_weight, value_weight, out_weight, passage_length
):
    dec, inner = queries.shape
    block, width = passages.shape
    half = inner // 2
    n_pass = passage_length.shape[0]
    number = (n_pass - 1) * PASS_LEN + 2 * SHORT_LEN
    n_z = n_rows // 4
    slots = 2 * n_z
    chunks = width // OUT_CHUNK
    bf16 = jnp.bfloat16
    dma = pltpu.SemaphoreType.DMA
    vmem = pl.BlockSpec(memory_space=pltpu.VMEM)
    anywhere = pl.BlockSpec(memory_space=pl.ANY)
    n_sends = 2 * (n_z - 1) + 2 * n_z + 1 + (slots - 1) + 3 * (slots - 1)
    return pl.pallas_call(
        functools.partial(kernel, n_rows, n_heads),
        out_shape=jax.ShapeDtypeStruct((dec, width), bf16),
        in_specs=[
            pl.BlockSpec(memory_space=pltpu.SMEM),
            anywhere,
            anywhere,
            vmem,
            anywhere,
            anywhere,
            anywhere,
        ],
        out_specs=vmem,
        scratch_shapes=[
            pltpu.VMEM((block, width), bf16),
            pltpu.VMEM((n_rows * block, width), bf16),
            pltpu.VMEM((2 * dec, half), bf16),
            pltpu.VMEM((width, half), bf16),
            pltpu.VMEM((width, half), bf16),
            pltpu.VMEM((half, width), bf16),
            pltpu.VMEM((n_rows * block, half), bf16),
            pltpu.VMEM((n_rows * block, half), bf16),
            pltpu.VMEM(((n_z - 1) * 2 * block, half), jnp.float32),
            pltpu.VMEM(((n_z - 1) * 2 * block, half), jnp.float32),
            pltpu.VMEM((2, 2 * dec // SPLITS, number), jnp.float32),
            pltpu.VMEM((2, 2 * dec // SPLITS, number), bf16),
            pltpu.VMEM((2 * dec, half), bf16),
            pltpu.VMEM((dec, width), bf16),
            pltpu.VMEM((dec, width), bf16),
            pltpu.VMEM((dec, width), jnp.float32),
            pltpu.VMEM((n_heads, dec, width), bf16),
            dma((2,)),
            dma((3, LOADS)),
            dma((n_sends,)),
            dma((slots, 2, 3)),
            dma((2,)),
            dma((2, SPLITS, chunks)),
            dma((2, SPLITS, n_heads - 1, chunks)),
        ],
        compiler_params=pltpu.CompilerParams(
            collective_id=0, has_side_effects=True, vmem_limit_bytes=40 * 1024 * 1024
        ),
    )(
        *(
            pltpu.with_memory_space_constraint(array, pltpu.HBM)
            for array in (
                passage_length,
                queries,
                passages,
                enc_gain,
                key_weight,
                value_weight,
                out_weight,
            )
        )
    )


def solution(mesh):
    return jax.shard_map(
        functools.partial(on_device, mesh.shape["rows"], mesh.shape["heads"]),
        mesh=mesh,
        in_specs=(
            P(("groups", "rows"), "heads"),
            P(("groups", "rows"), None),
            P(),
            P(None, "heads"),
            P(None, "heads"),
            P("heads", None),
            P("groups"),
        ),
        out_specs=P(("groups", "rows"), None),
        check_vma=False,
    )
```

time: 45.6 us -> 38 us (0.83)
  Pallas kernels: 43.7 us -> 37.1 us
  local copies, waits for them, and re-layouts: 1.67 us -> 0.71 us
    pallas_call x1, Pallas kernels: 43.7 us -> 37.1 us  [on_device(): pl.pallas_call(functools.partial(kernel, n_rows, n_heads), out_shape=jax....]
    unnamed x1, local copies, waits for them, and re-layouts: 1.67 us -> 0.71 us
where the time goes in v1:
time: 38 us; the launch traced here: 37.8 us
  Pallas kernels  37.1 us (98%)
  local copies, waits for them, and re-layouts  0.71 us (2%)
    pallas_call x1, Pallas kernels, on_device(): pl.pallas_call(functools.partial(kernel, n_rows, n_heads), out_shape=jax....  37.1 us

profile of v1, /device:TPU:0, one launch (start us, length us, event | category | flops | bytes accessed | tf_op | source)
XLA Modules:
  0.0 37.8 jit_solution(16069643675079098538)
XLA Ops:
  0.0 37.1 %shard_map.73 = bf16[128,1024]{1,0:T(8,128)(2,1)S(1)} custom-call(s32[3]{0:T(128)} %length_ref.1, bf16[128,4096]{1,0:T(8,128)(2,1)} %queries_ref.1, bf16[48,1024]{1,0:T(8,128)(2,1)} %passages_ref.1, bf16[1024]{0:T(1024)(128)(2,1)} %gain_ref.1, bf16[1024,4096]{1,0:T(8,128)(2,1)} %key_ref.1, bf16[1024,4096]{1,0:T(8,128)(2,1)} %value_ref.1, ...), custom_call_target="tpu_custom_call" | custom-call | tf_op jit(solution)/shard_map/pallas_call | solution.py:476
  37.1 0.7 %copy.9 = bf16[128,1024]{1,0:T(8,128)(2,1)} copy(bf16[128,1024]{1,0:T(8,128)(2,1)S(1)} %shard_map.73) | data formatting | bytes 524288

commit v2 on v1

--- a/solution.py
+++ b/solution.py
@@ -18,6 +18,8 @@
 ROW_BLOCK = 16
 GIVE, SHARED, REST = 0, 1, 2
 SPLITS = 2
+PARTS = (2, 2, 1)
+EACH = (3, 2, 3)
 
 
 def flip(index, bits):
@@ -182,10 +184,12 @@
         view = unit_of(slot, c, kind)
         pltpu.make_async_copy(view, view, recv_sem.at[slot, c, kind]).wait()
 
-    for kind in (GIVE, SHARED):
+    def send_own(kind):
         for d in range(n_z - 1, 0, -1):
             send_unit(0, kind, z_peers[d - 1], slot_of(0, d), kind)
         send_unit(0, kind, across_y, slot_of(1, 0), kind)
+
+    send_own(GIVE)
     send(whole_of(0, core), whole_of(0, core), next_sem(), recv_sem.at[0, core, 0], partner)
     send(
         queries_ref.at[:, theirs], query_buf.at[dec : 2 * dec], query_sem.at[0], query_sem.at[1], partner
@@ -264,8 +268,12 @@
         for event in events:
             event()
 
-    def pieces_of(work, slots):
-        return [functools.partial(work, slots, g) for g in range(groups)]
+    def pieces_of(work, slots, parts):
+        def piece(part):
+            for g in range(groups * part // parts, groups * (part + 1) // parts):
+                work(slots, g)
+
+        return [functools.partial(piece, part) for part in range(parts)]
 
     near = list(range(n_z - 1, 0, -1))
     line = [slot_of(0, d) for d in near]
@@ -278,28 +286,31 @@
                 await_unit(slot, 1 - core, kind)
 
     R = functools.partial
-    relay(beside, GIVE, False)
     view = whole_of(0, 1 - core)
     pltpu.make_async_copy(view, view, recv_sem.at[0, 1 - core, 0]).wait()
-    events = [R(relay, beside, SHARED, False)]
-    events += [R(relay, s, GIVE, True) for s in line]
-    events += [R(relay, beside, REST, False)]
-    events += [R(relay, s, SHARED, True) for s in line]
-    interleave(pieces_of(project, [0]), events, 1)
+    interleave(pieces_of(project, [0], 2), [R(send_own, SHARED)], 1)
+    relay(beside, GIVE, False)
+    for s in line:
+        relay(s, GIVE, True)
+    relay(beside, SHARED, False)
+    relay(beside, REST, False)
+    for s in line:
+        relay(s, SHARED, True)
     from_partner([beside], (GIVE, SHARED, REST))
     events = []
     for s, o in zip(line, other):
         events += [R(relay, o, GIVE, False), R(relay, s, REST, False)]
-    interleave(pieces_of(project, [beside]), events, 2)
-    from_partner(line, (GIVE, SHARED, REST))
+    interleave(pieces_of(project, [beside], PARTS[0]), events, EACH[0])
+    from_partner(line, (GIVE, SHARED))
     events = [R(relay, o, SHARED, False) for o in other]
-    events += [R(relay, o, REST, False) for o in other]
-    interleave(pieces_of(project, line[::-1]), events, 1)
+    interleave(pieces_of(project_main, line[::-1], PARTS[1]), events, EACH[1])
+    from_partner(line, (REST,))
+    events = [R(relay, o, REST, False) for o in other]
+    interleave(pieces_of(project_rest, line[::-1], PARTS[2]), events, EACH[2])
     from_partner(other, (GIVE, SHARED))
-    interleave(pieces_of(project_main, other[::-1]), [], 1)
+    interleave(pieces_of(project_main, other[::-1], 1), [], 1)
     from_partner(other, (REST,))
-    for piece in pieces_of(project_rest, other[::-1]):
-        piece()
+    interleave(pieces_of(project_rest, other[::-1], 1), [], 1)
 
     lengths = [length_ref[p] for p in range(n_pass)]
     short_at = jnp.int32(0)

time: 38 us -> 36.9 us (0.971)
  Pallas kernels: 37.1 us -> 36 us
    pallas_call x1, Pallas kernels: 37.1 us -> 36 us  [on_device(): pl.pallas_call(functools.partial(kernel, n_rows, n_heads), out_shape=jax....]
where the time goes in v2:
time: 36.9 us; the launch traced here: 36.7 us
  Pallas kernels  36 us (98%)
  local copies, waits for them, and re-layouts  0.71 us (2%)
    pallas_call x1, Pallas kernels, on_device(): pl.pallas_call(functools.partial(kernel, n_rows, n_heads), out_shape=jax....  36 us

profile of v2, /device:TPU:0, one launch (start us, length us, event | category | flops | bytes accessed | tf_op | source)
XLA Modules:
  0.0 36.7 jit_solution(12299243885613479092)
XLA Ops:
  0.0 36.0 %shard_map.73 = bf16[128,1024]{1,0:T(8,128)(2,1)S(1)} custom-call(s32[3]{0:T(128)} %length_ref.1, bf16[128,4096]{1,0:T(8,128)(2,1)} %queries_ref.1, bf16[48,1024]{1,0:T(8,128)(2,1)} %passages_ref.1, bf16[1024]{0:T(1024)(128)(2,1)} %gain_ref.1, bf16[1024,4096]{1,0:T(8,128)(2,1)} %key_ref.1, bf16[1024,4096]{1,0:T(8,128)(2,1)} %value_ref.1, ...), custom_call_target="tpu_custom_call" | custom-call | tf_op jit(solution)/shard_map/pallas_call | solution.py:487
  36.0 0.7 %copy.9 = bf16[128,1024]{1,0:T(8,128)(2,1)} copy(bf16[128,1024]{1,0:T(8,128)(2,1)S(1)} %shard_map.73) | data formatting | bytes 524288

commit v3 on v2

--- a/solution.py
+++ b/solution.py
@@ -18,8 +18,8 @@
 ROW_BLOCK = 16
 GIVE, SHARED, REST = 0, 1, 2
 SPLITS = 2
-PARTS = (2, 2, 1)
-EACH = (3, 2, 3)
+PARTS = 2
+EACH = 3
 
 
 def flip(index, bits):
@@ -130,8 +130,6 @@
 
     give_at = pl.multiple_of(side * (width - quarter), 128)
     rest_at = pl.multiple_of((1 - side) * (width - quarter), 128)
-    main_at = pl.multiple_of(side * quarter, 128)
-    main_cols = pl.ds(main_at, width - quarter)
     rest_cols = pl.ds(rest_at, quarter)
     cols_of = {GIVE: pl.ds(give_at, quarter), SHARED: pl.ds(quarter, middle), REST: rest_cols}
 
@@ -187,7 +185,9 @@
     def send_own(kind):
         for d in range(n_z - 1, 0, -1):
             send_unit(0, kind, z_peers[d - 1], slot_of(0, d), kind)
-        send_unit(0, kind, across_y, slot_of(1, 0), kind)
+        if kind == GIVE:
+            for early in (GIVE, SHARED):
+                send_unit(0, early, across_y, slot_of(1, 0), early)
 
     send_own(GIVE)
     send(whole_of(0, core), whole_of(0, core), next_sem(), recv_sem.at[0, core, 0], partner)
@@ -238,25 +238,20 @@
             jnp.dot(chunk, value_w[:, cols], preferred_element_type=f32),
         )
 
-    def project_main(slots, g):
+    def project_part(which, cols_in, first, last, slots, g):
         cols = slice(g * GROUP, (g + 1) * GROUP)
-        chunk = rows[rows_in(slots), main_cols]
+        chunk = rows[rows_in(slots), cols_in]
         here = slice(0, len(slots) * 2 * block)
-        key_sum[here, cols] = jnp.dot(chunk, key_w[main_cols, cols], preferred_element_type=f32)
-        value_sum[here, cols] = jnp.dot(chunk, value_w[main_cols, cols], preferred_element_type=f32)
-
-    def project_rest(slots, g):
-        cols = slice(g * GROUP, (g + 1) * GROUP)
-        chunk = rows[rows_in(slots), rest_cols]
-        here = slice(0, len(slots) * 2 * block)
-        keep(
-            slots,
-            cols,
-            key_sum[here, cols]
-            + jnp.dot(chunk, key_w[rest_cols, cols], preferred_element_type=f32),
-            value_sum[here, cols]
-            + jnp.dot(chunk, value_w[rest_cols, cols], preferred_element_type=f32),
-        )
+        made_keys = jnp.dot(chunk, key_w[cols_in, cols], preferred_element_type=f32)
+        made_values = jnp.dot(chunk, value_w[cols_in, cols], preferred_element_type=f32)
+        if not first:
+            made_keys += key_sum[which, here, cols]
+            made_values += value_sum[which, here, cols]
+        if last:
+            keep(slots, cols, made_keys, made_values)
+        else:
+            key_sum[which, here, cols] = made_keys
+            value_sum[which, here, cols] = made_values
 
     def interleave(pieces, events, each):
         events = list(events)
@@ -289,28 +284,36 @@
     view = whole_of(0, 1 - core)
     pltpu.make_async_copy(view, view, recv_sem.at[0, 1 - core, 0]).wait()
     interleave(pieces_of(project, [0], 2), [R(send_own, SHARED)], 1)
+    ahead, across = line[::-1], other[::-1]
+    main_cols = pl.ds(pl.multiple_of(side * quarter, 128), width - quarter)
+    late_cols = pl.ds(pl.multiple_of((1 - side) * quarter, 128), width - quarter)
     relay(beside, GIVE, False)
     for s in line:
         relay(s, GIVE, True)
     relay(beside, SHARED, False)
+    from_partner(line, (GIVE,))
+    interleave(pieces_of(R(project_part, 0, cols_of[GIVE], True, False), ahead, 1), [], 1)
+    from_partner([beside], (GIVE, SHARED))
+    interleave(pieces_of(R(project_part, 1, main_cols, True, False), [beside], 1), [], 1)
+    for o in other:
+        relay(o, GIVE, False)
     relay(beside, REST, False)
     for s in line:
         relay(s, SHARED, True)
-    from_partner([beside], (GIVE, SHARED, REST))
-    events = []
-    for s, o in zip(line, other):
-        events += [R(relay, o, GIVE, False), R(relay, s, REST, False)]
-    interleave(pieces_of(project, [beside], PARTS[0]), events, EACH[0])
-    from_partner(line, (GIVE, SHARED))
-    events = [R(relay, o, SHARED, False) for o in other]
-    interleave(pieces_of(project_main, line[::-1], PARTS[1]), events, EACH[1])
-    from_partner(line, (REST,))
+    for s in line:
+        relay(s, REST, False)
+    from_partner([beside], (REST,))
+    interleave(pieces_of(R(project_part, 1, cols_of[REST], False, True), [beside], 1), [], 1)
+    from_partner(other, (GIVE,))
+    interleave(pieces_of(R(project_part, 1, cols_of[GIVE], True, False), across, 1), [], 1)
+    from_partner(line, (SHARED, REST))
     events = [R(relay, o, REST, False) for o in other]
-    interleave(pieces_of(project_rest, line[::-1], PARTS[2]), events, EACH[2])
-    from_partner(other, (GIVE, SHARED))
-    interleave(pieces_of(project_main, other[::-1], 1), [], 1)
+    events += [R(relay, o, SHARED, False) for o in other]
+    interleave(pieces_of(R(project_part, 0, late_cols, False, True), ahead, PARTS), events, EACH)
     from_partner(other, (REST,))
-    interleave(pieces_of(project_rest, other[::-1], 1), [], 1)
+    interleave(pieces_of(R(project_part, 1, cols_of[REST], False, False), across, 1), [], 1)
+    from_partner(other, (SHARED,))
+    interleave(pieces_of(R(project_part, 1, cols_of[SHARED], False, True), across, 1), [], 1)
 
     lengths = [length_ref[p] for p in range(n_pass)]
     short_at = jnp.int32(0)
@@ -506,8 +509,8 @@
             pltpu.VMEM((half, width), bf16),
             pltpu.VMEM((n_rows * block, half), bf16),
             pltpu.VMEM((n_rows * block, half), bf16),
-            pltpu.VMEM(((n_z - 1) * 2 * block, half), jnp.float32),
-            pltpu.VMEM(((n_z - 1) * 2 * block, half), jnp.float32),
+            pltpu.VMEM((2, (n_z - 1) * 2 * block, half), jnp.float32),
+            pltpu.VMEM((2, (n_z - 1) * 2 * block, half), jnp.float32),
             pltpu.VMEM((2, 2 * dec // SPLITS, number), jnp.float32),
             pltpu.VMEM((2, 2 * dec // SPLITS, number), bf16),
             pltpu.VMEM((2 * dec, half), bf16),

time: 36.9 us -> 35.1 us (0.951)
  Pallas kernels: 36 us -> 34.2 us
    pallas_call x1, Pallas kernels: 36 us -> 34.2 us  [on_device(): pl.pallas_call(functools.partial(kernel, n_rows, n_heads), out_shape=jax....]
where the time goes in v3:
time: 35.1 us; the launch traced here: 34.9 us
  Pallas kernels  34.2 us (97%)
  local copies, waits for them, and re-layouts  0.71 us (2%)
    pallas_call x1, Pallas kernels, on_device(): pl.pallas_call(functools.partial(kernel, n_rows, n_heads), out_shape=jax....  34.2 us
    unnamed x1, local copies, waits for them, and re-layouts  0.71 us

profile of v3, /device:TPU:0, one launch (start us, length us, event | category | flops | bytes accessed | tf_op | source)
XLA Modules:
  0.0 34.9 jit_solution(2377115466837688137)
XLA Ops:
  0.0 34.2 %shard_map.73 = bf16[128,1024]{1,0:T(8,128)(2,1)S(1)} custom-call(s32[3]{0:T(128)} %length_ref.1, bf16[128,4096]{1,0:T(8,128)(2,1)} %queries_ref.1, bf16[48,1024]{1,0:T(8,128)(2,1)} %passages_ref.1, bf16[1024]{0:T(1024)(128)(2,1)} %gain_ref.1, bf16[1024,4096]{1,0:T(8,128)(2,1)} %key_ref.1, bf16[1024,4096]{1,0:T(8,128)(2,1)} %value_ref.1, ...), custom_call_target="tpu_custom_call" | custom-call | tf_op jit(solution)/shard_map/pallas_call | solution.py:490
  34.2 0.7 %copy.9 = bf16[128,1024]{1,0:T(8,128)(2,1)} copy(bf16[128,1024]{1,0:T(8,128)(2,1)S(1)} %shard_map.73) | data formatting | bytes 524288

commit v4 on v3

--- a/solution.py
+++ b/solution.py
@@ -34,14 +34,16 @@
 def kernel(
     n_rows,
     n_heads,
-    length_ref,
+    length_hbm,
     queries_ref,
     passages_ref,
-    gain_ref,
+    gain_hbm,
     key_ref,
     value_ref,
     outw_ref,
     out_ref,
+    length_ref,
+    gain_ref,
     own_raw,
     rows,
     query_buf,
@@ -95,6 +97,10 @@
 
     own_rows = pltpu.make_async_copy(passages_ref, own_raw, local_sem.at[0])
     own_rows.start()
+    own_gain = pltpu.make_async_copy(gain_hbm, gain_ref, local_sem.at[2])
+    own_gain.start()
+    own_length = pltpu.make_async_copy(length_hbm, length_ref, local_sem.at[3])
+    own_length.start()
     barrier = pltpu.get_barrier_semaphore()
     peers = z_peers + [across_y, partner] + x_peers
     for peer in peers:
@@ -140,6 +146,7 @@
         return rows.at[place(slot, c)]
 
     own_rows.wait()
+    own_gain.wait()
     for triple in loads:
         triple[0].start()
         triple[1].start()
@@ -315,6 +322,7 @@
     from_partner(other, (SHARED,))
     interleave(pieces_of(R(project_part, 1, cols_of[SHARED], False, True), across, 1), [], 1)
 
+    own_length.wait()
     lengths = [length_ref[p] for p in range(n_pass)]
     short_at = jnp.int32(0)
     full_at = jnp.int32(0)
@@ -491,16 +499,18 @@
         functools.partial(kernel, n_rows, n_heads),
         out_shape=jax.ShapeDtypeStruct((dec, width), bf16),
         in_specs=[
-            pl.BlockSpec(memory_space=pltpu.SMEM),
-            anywhere,
-            anywhere,
-            vmem,
+            anywhere,
+            anywhere,
+            anywhere,
+            anywhere,
             anywhere,
             anywhere,
             anywhere,
         ],
         out_specs=vmem,
         scratch_shapes=[
+            pltpu.SMEM((n_pass,), jnp.int32),
+            pltpu.VMEM((width,), bf16),
             pltpu.VMEM((block, width), bf16),
             pltpu.VMEM((n_rows * block, width), bf16),
             pltpu.VMEM((2 * dec, half), bf16),
@@ -518,7 +528,7 @@
             pltpu.VMEM((dec, width), bf16),
             pltpu.VMEM((dec, width), jnp.float32),
             pltpu.VMEM((n_heads, dec, width), bf16),
-            dma((2,)),
+            dma((4,)),
             dma((3, LOADS)),
             dma((n_sends,)),
             dma((slots, 2, 3)),

time: 35.1 us -> 34.5 us (0.983)
  Pallas kernels: 34.2 us -> 33.7 us
    pallas_call x1, Pallas kernels: 34.2 us -> 33.7 us  [on_device(): pl.pallas_call(functools.partial(kernel, n_rows, n_heads), out_shape=jax....]
where the time goes in v4:
time: 34.5 us; the launch traced here: 34.4 us
  Pallas kernels  33.7 us (98%)
  local copies, waits for them, and re-layouts  0.71 us (2%)
    pallas_call x1, Pallas kernels, on_device(): pl.pallas_call(functools.partial(kernel, n_rows, n_heads), out_shape=jax....  33.7 us
    unnamed x1, local copies, waits for them, and re-layouts  0.71 us

profile of v4, /device:TPU:0, one launch (start us, length us, event | category | flops | bytes accessed | tf_op | source)
XLA Modules:
  0.0 34.4 jit_solution(14265279370201237866)
XLA Ops:
  0.0 33.7 %shard_map.73 = bf16[128,1024]{1,0:T(8,128)(2,1)S(1)} custom-call(s32[3]{0:T(128)} %length_hbm.1, bf16[128,4096]{1,0:T(8,128)(2,1)} %queries_ref.1, bf16[48,1024]{1,0:T(8,128)(2,1)} %passages_ref.1, bf16[1024]{0:T(1024)(128)(2,1)} %gain_hbm.1, bf16[1024,4096]{1,0:T(8,128)(2,1)} %key_ref.1, bf16[1024,4096]{1,0:T(8,128)(2,1)} %value_ref.1, ...), custom_call_target="tpu_custom_call" | custom-call | tf_op jit(solution)/shard_map/pallas_call | solution.py:498
  33.7 0.7 %copy.9 = bf16[128,1024]{1,0:T(8,128)(2,1)} copy(bf16[128,1024]{1,0:T(8,128)(2,1)S(1)} %shard_map.73) | data formatting | bytes 524288

commit v5 on v4

--- a/solution.py
+++ b/solution.py
@@ -290,7 +290,8 @@
     R = functools.partial
     view = whole_of(0, 1 - core)
     pltpu.make_async_copy(view, view, recv_sem.at[0, 1 - core, 0]).wait()
-    interleave(pieces_of(project, [0], 2), [R(send_own, SHARED)], 1)
+    send_own(SHARED)
+    interleave(pieces_of(project, [0], 1), [], 1)
     ahead, across = line[::-1], other[::-1]
     main_cols = pl.ds(pl.multiple_of(side * quarter, 128), width - quarter)
     late_cols = pl.ds(pl.multiple_of((1 - side) * quarter, 128), width - quarter)

time: 34.5 us -> 36.2 us (1.049)
  Pallas kernels: 33.7 us -> 35.3 us
    pallas_call x1, Pallas kernels: 33.7 us -> 35.3 us  [on_device(): pl.pallas_call(functools.partial(kernel, n_rows, n_heads), out_shape=jax....]
where the time goes in v5:
time: 36.2 us; the launch traced here: 36 us
  Pallas kernels  35.3 us (98%)
  local copies, waits for them, and re-layouts  0.71 us (2%)
    pallas_call x1, Pallas kernels, on_device(): pl.pallas_call(functools.partial(kernel, n_rows, n_heads), out_shape=jax....  35.3 us

profile of v5, /device:TPU:0, one launch (start us, length us, event | category | flops | bytes accessed | tf_op | source)
XLA Modules:
  0.0 36.0 jit_solution(7255637138758645487)
XLA Ops:
  0.0 35.3 %shard_map.73 = bf16[128,1024]{1,0:T(8,128)(2,1)S(1)} custom-call(s32[3]{0:T(128)} %length_hbm.1, bf16[128,4096]{1,0:T(8,128)(2,1)} %queries_ref.1, bf16[48,1024]{1,0:T(8,128)(2,1)} %passages_ref.1, bf16[1024]{0:T(1024)(128)(2,1)} %gain_hbm.1, bf16[1024,4096]{1,0:T(8,128)(2,1)} %key_ref.1, bf16[1024,4096]{1,0:T(8,128)(2,1)} %value_ref.1, ...), custom_call_target="tpu_custom_call" | custom-call | tf_op jit(solution)/shard_map/pallas_call | solution.py:499
  35.3 0.7 %copy.9 = bf16[128,1024]{1,0:T(8,128)(2,1)} copy(bf16[128,1024]{1,0:T(8,128)(2,1)S(1)} %shard_map.73) | data formatting | bytes 524288
